TPU v7x, 256 devices: a whole 4x4x8 slice. The times are simulated.
256 devices in a mesh: seq: 16 (over z, core), head: 8 (over x_lo, y), batch: 2 (over x_hi).
Axes of the slice: x: 4 (x_hi: 2, x_lo: 2; x = x_hi * 2 + x_lo), y: 4, z: 8, core: 2. Of those that a mesh axis runs over, the one named last changes fastest.
Arguments:
- queries: bfloat16 [8192, 4096], P(('batch', 'seq'), 'head'), parts along dimension 0, may hold values from -16 to 16, as said below
- key_rows: bfloat16 [8192, 1024], P(('batch', 'seq'), 'head'), parts along dimension 0, may hold values from -16 to 16
- value_rows: bfloat16 [8192, 1024], P(('batch', 'seq'), 'head'), parts along dimension 0, may hold values from -6 to 6
- out_grad: bfloat16 [8192, 4096], P(('batch', 'seq'), 'head'), parts along dimension 0, may hold values from -6 to 6
- tile_ids: int32 [64], P('batch'), parts along dimension 0, may hold values from 0 to 31, each once
- tile_mask: int32 [64, 32], P('batch'), parts along dimension 0, may hold values from 0 to 1, as said below
Outputs:
- attended: bfloat16 [8192, 4096], P(('batch', 'seq'), 'head'), parts along dimension 0
- query_grad: float32 [8192, 4096], P(('batch', 'seq'), 'head'), parts along dimension 0
- key_grad: float32 [8192, 1024], P(('batch', 'seq'), 'head'), parts along dimension 0
- value_grad: float32 [8192, 1024], P(('batch', 'seq'), 'head'), parts along dimension 0
There are 2 independent parts, one for each index of `batch`. A program takes and returns all parts, laid end to end along the dimension named above; each array names one. Nothing has to cross between parts.
Inputs may be any that keep to these rules, and one draw needn't show every extreme that they name: `queries`: in the hidden draw a few query rows equal scaled key rows of the same tile. `tile_mask`: 1 only where the key tile's index is at most the query tile's; 1 on the diagonal.
All inputs are finite; a program needn't handle non-finite values.
Results may differ from a plain program's by a relative error of at most 0.03.
Values may be sent and summed in bfloat16 or wider, within the bound.
A program may use at most 64 MiB of HBM per device.

v0:
```python
import math

import jax
import jax.numpy as jnp
from jax import lax
from jax.sharding import PartitionSpec as P

HD = 128
TILE = 128


far_below = -1e30


def tile_allowed(tile_mask, query_tiles, key_tiles):
    table = jnp.take(jnp.take(tile_mask, query_tiles, axis=0), key_tiles, axis=1) == 1
    same_tile = query_tiles[:, None] == key_tiles[None, :]
    inside = lax.broadcasted_iota(jnp.int32, (TILE, TILE), 0) >= lax.broadcasted_iota(
        jnp.int32, (TILE, TILE), 1
    )
    full = table[:, None, :, None] & (
        jnp.logical_not(same_tile)[:, None, :, None] | inside[None, :, None, :]
    )
    return full.reshape(query_tiles.shape[0] * TILE, key_tiles.shape[0] * TILE)


def sub_blocks(row_total, limit):
    block_rows = math.gcd(row_total, limit)
    return (block_rows, row_total // block_rows)


def per_device(queries, key_rows, value_rows, out_grad, tile_ids, tile_mask):
    row_count = queries.shape[0]
    group_count = key_rows.shape[1] // HD
    head_count = queries.shape[1] // (group_count * HD)
    factor = HD ** (-0.5)
    my_rank = lax.axis_index("seq")
    limit = 1024
    query_heads = queries.reshape(row_count, group_count, head_count, HD)
    grad_heads = out_grad.reshape(row_count, group_count, head_count, HD)
    query_tiles = lax.dynamic_slice_in_dim(
        tile_ids, my_rank * (row_count // TILE), row_count // TILE
    )

    def block_mask(first_row, row_total):
        key_tiles = lax.dynamic_slice_in_dim(tile_ids, first_row // TILE, row_total // TILE)
        return tile_allowed(tile_mask, query_tiles, key_tiles)

    def masked_scores(key_block, allowed):
        scores = (
            jnp.einsum("qghd,kgd->ghqk", query_heads, key_block, preferred_element_type=jnp.float32)
            * factor
        )
        return jnp.where(allowed[None, None], scores, far_below)

    def forward_block(carried, key_block, value_block, first_row):
        allowed = block_mask(first_row, key_block.shape[0])
        row_max, denominator, weighted = carried
        scores = masked_scores(key_block, allowed)
        new_max = jnp.maximum(row_max, jnp.max(scores, axis=-1))
        shrink = jnp.exp(row_max - new_max)
        softmax_terms = jnp.where(allowed[None, None], jnp.exp(scores - new_max[..., None]), 0.0)
        denominator = denominator * shrink + jnp.sum(softmax_terms, axis=-1)
        weighted = weighted * shrink[..., None] + jnp.einsum(
            "ghqk,kgd->ghqd",
            softmax_terms.astype(jnp.bfloat16),
            value_block,
            preferred_element_type=jnp.float32,
        )
        return (new_max, denominator, weighted)

    stat_shape = (group_count, head_count, row_count)
    initial = (
        jnp.full(stat_shape, far_below, jnp.float32),
        jnp.zeros(stat_shape, jnp.float32),
        jnp.zeros(stat_shape + (HD,), jnp.float32),
    )
    key_piece = lax.all_gather(key_rows, "seq", axis=0, tiled=True)
    value_piece = lax.all_gather(value_rows, "seq", axis=0, tiled=True)
    block_rows, number = sub_blocks(key_piece.shape[0], limit)

    def forward_advance(position, current):
        key_block = lax.dynamic_slice_in_dim(key_piece, position * block_rows, block_rows).reshape(
            block_rows, group_count, HD
        )
        value_block = lax.dynamic_slice_in_dim(
            value_piece, position * block_rows, block_rows
        ).reshape(block_rows, group_count, HD)
        return forward_block(current, key_block, value_block, position * block_rows)

    row_max, denominator, weighted = lax.fori_loop(0, number, forward_advance, initial)
    attended_heads = jnp.transpose(weighted / denominator[..., None], (2, 0, 1, 3))
    attended = attended_heads.reshape(row_count, group_count * head_count * HD).astype(jnp.bfloat16)
    log_total = row_max + jnp.log(denominator)
    row_delta = jnp.transpose(
        jnp.sum(
            grad_heads.astype(jnp.float32)
            * attended.reshape(row_count, group_count, head_count, HD).astype(jnp.float32),
            axis=-1,
        ),
        (1, 2, 0),
    )

    def backward_block(key_block, value_block, first_row):
        allowed = block_mask(first_row, key_block.shape[0])
        scores = masked_scores(key_block, allowed)
        softmax_terms = jnp.where(allowed[None, None], jnp.exp(scores - log_total[..., None]), 0.0)
        dprobs = jnp.einsum(
            "qghd,kgd->ghqk", grad_heads, value_block, preferred_element_type=jnp.float32
        )
        dscores = (softmax_terms * (dprobs - row_delta[..., None])).astype(jnp.bfloat16)
        query_part = (
            jnp.einsum("ghqk,kgd->qghd", dscores, key_block, preferred_element_type=jnp.float32)
            * factor
        )
        key_part = (
            jnp.einsum("ghqk,qghd->kgd", dscores, query_heads, preferred_element_type=jnp.float32)
            * factor
        )
        value_part = jnp.einsum(
            "ghqk,qghd->kgd",
            softmax_terms.astype(jnp.bfloat16),
            grad_heads,
            preferred_element_type=jnp.float32,
        )
        key_flat = key_part.reshape(key_block.shape[0], group_count * HD)
        value_flat = value_part.reshape(key_block.shape[0], group_count * HD)
        return (query_part, jnp.concatenate([key_flat, value_flat], axis=-1))

    gathered_keys, gathered_values = (
        lax.all_gather(key_rows, "seq", axis=0, tiled=True),
        lax.all_gather(value_rows, "seq", axis=0, tiled=True),
    )
    sweep_block_rows, number = sub_blocks(gathered_keys.shape[0], limit)

    def sweep_advance(query_sum, position):
        key_block = lax.dynamic_slice_in_dim(
            gathered_keys, position * sweep_block_rows, sweep_block_rows
        ).reshape(sweep_block_rows, group_count, HD)
        value_block = lax.dynamic_slice_in_dim(
            gathered_values, position * sweep_block_rows, sweep_block_rows
        ).reshape(sweep_block_rows, group_count, HD)
        query_part, key_value = backward_block(
            key_block, value_block, 0 + position * sweep_block_rows
        )
        return (query_sum + query_part, key_value)

    query_sum, stacked = lax.scan(
        sweep_advance,
        jnp.zeros((row_count, group_count, head_count, HD), jnp.float32),
        jnp.arange(number, dtype=jnp.int32),
    )
    query_sum, key_terms = (
        query_sum,
        stacked.reshape(gathered_keys.shape[0], 2 * group_count * HD),
    )
    own_terms = lax.psum_scatter(
        key_terms.astype(jnp.bfloat16), "seq", scatter_dimension=0, tiled=True
    ).astype(jnp.float32)
    query_grad = query_sum.reshape(row_count, group_count * head_count * HD)
    width = group_count * HD
    return (attended, query_grad, own_terms[:, :width], own_terms[:, width:])


def solution(mesh):
    return jax.shard_map(
        per_device,
        mesh=mesh,
        in_specs=(
            P(("batch", "seq"), "head"),
            P(("batch", "seq"), "head"),
            P(("batch", "seq"), "head"),
            P(("batch", "seq"), "head"),
            P("batch"),
            P("batch", None),
        ),
        out_specs=(
            P(("batch", "seq"), "head"),
            P(("batch", "seq"), "head"),
            P(("batch", "seq"), "head"),
            P(("batch", "seq"), "head"),
        ),
        check_vma=False,
    )
```

profile of v0, /device:TPU:2, one launch (start us, length us, event | category | flops | bytes accessed | tf_op | source)
XLA Modules:
  0.0 242.3 jit_solution(15315642816570585273)
XLA Ops:
  12.6 38.7 %all-gather.3.cloned.1.call-done = bf16[4096,128]{1,0:T(8,128)(2,1)} async-done(((bf16[256,128]{1,0:T(8,128)(2,1)}), bf16[4096,128]{1,0:T(8,128)(2,1)}) %all-gather.3.cloned.1.call-update) | async-done | bytes 1048592 | tf_op jit(solution)/shard_map/all_gather | solution.py:78
  51.4 39.0 %all-gather.5.cloned.1.call-done = bf16[4096,128]{1,0:T(8,128)(2,1)} async-done(((bf16[256,128]{1,0:T(8,128)(2,1)}), bf16[4096,128]{1,0:T(8,128)(2,1)}) %all-gather.5.cloned.1.call-update) | async-done | bytes 1048592 | tf_op jit(solution)/shard_map/all_gather | solution.py:79
  90.3 30.9 %while.35 = (s32[]{:T(128)}, f32[1,4,256]{2,1,0:T(4,128)S(1)}, f32[1,4,256]{2,1,0:T(4,128)S(1)}, f32[1,4,256,128]{3,2,1,0:T(8,128)S(1)}, s32[32]{0:T(128)}, /*in...) while((s32[]{:T(128)}, f32[1,4,256]{2,1,0:T(4,128)S(1)}, ...), condition=%wide.region_3.6_spmd.clone, body=%wide.region_0.5_spmd.clone.sunk | while | flops 551443584 | bytes 16618426 | solution.py:91
  92.7 1.8 fusion.100
  95.5 2.4 %fusion.103 = f32[1,4,256,128]{3,2,1,0:T(8,128)S(1)} fusion(f32[1024,256,4]{1,0,2:T(8,128)S(1)} %get-tuple-element.745, f32[4,256]{1,0:T(4,128)S(1)} %bitcast.245, pred[256,1024]{0,1:T(8,128)(4,1)S(1)} %copy.70, f32[1,4,256,128]{3,2,1,0:T(8,128)S(1)} %get-tuple-element.783, bf16[4096,128]{1,0:T(8,128)(2,1)} %get-tuple-element.807, ...), kind=kOutput, calls=%fused_computation.12.clone.1 | convolution fusion | flops 274071552 | bytes 5775365 | tf_op jit(solution)/shard_map/while/body/eval_jaxpr/ghqk,kgd->ghqd/dot_general | solution.py:64
  100.4 1.8 fusion.100
  103.3 2.4 %fusion.103 = f32[1,4,256,128]{3,2,1,0:T(8,128)S(1)} fusion(f32[1024,256,4]{1,0,2:T(8,128)S(1)} %get-tuple-element.745, f32[4,256]{1,0:T(4,128)S(1)} %bitcast.245, pred[256,1024]{0,1:T(8,128)(4,1)S(1)} %copy.70, f32[1,4,256,128]{3,2,1,0:T(8,128)S(1)} %get-tuple-element.783, bf16[4096,128]{1,0:T(8,128)(2,1)} %get-tuple-element.807, ...), kind=kOutput, calls=%fused_computation.12.clone.1 | convolution fusion | flops 274071552 | bytes 5775365 | tf_op jit(solution)/shard_map/while/body/eval_jaxpr/ghqk,kgd->ghqd/dot_general | solution.py:64
  108.2 1.8 fusion.100
  111.0 2.4 %fusion.103 = f32[1,4,256,128]{3,2,1,0:T(8,128)S(1)} fusion(f32[1024,256,4]{1,0,2:T(8,128)S(1)} %get-tuple-element.745, f32[4,256]{1,0:T(4,128)S(1)} %bitcast.245, pred[256,1024]{0,1:T(8,128)(4,1)S(1)} %copy.70, f32[1,4,256,128]{3,2,1,0:T(8,128)S(1)} %get-tuple-element.783, bf16[4096,128]{1,0:T(8,128)(2,1)} %get-tuple-element.807, ...), kind=kOutput, calls=%fused_computation.12.clone.1 | convolution fusion | flops 274071552 | bytes 5775365 | tf_op jit(solution)/shard_map/while/body/eval_jaxpr/ghqk,kgd->ghqd/dot_general | solution.py:64
  115.9 1.8 fusion.100
  118.8 2.4 %fusion.103 = f32[1,4,256,128]{3,2,1,0:T(8,128)S(1)} fusion(f32[1024,256,4]{1,0,2:T(8,128)S(1)} %get-tuple-element.745, f32[4,256]{1,0:T(4,128)S(1)} %bitcast.245, pred[256,1024]{0,1:T(8,128)(4,1)S(1)} %copy.70, f32[1,4,256,128]{3,2,1,0:T(8,128)S(1)} %get-tuple-element.783, bf16[4096,128]{1,0:T(8,128)(2,1)} %get-tuple-element.807, ...), kind=kOutput, calls=%fused_computation.12.clone.1 | convolution fusion | flops 274071552 | bytes 5775365 | tf_op jit(solution)/shard_map/while/body/eval_jaxpr/ghqk,kgd->ghqd/dot_general | solution.py:64
  121.6 49.8 %while.36 = (s32[]{:T(128)}, f32[256,1,4,128]{0,3,2,1:T(8,128)S(1)}, bf16[4,1024,256]{1,2,0:T(8,128)(2,1)}, s32[4]{0:T(128)S(1)}, bf16[4096,128]{1,0:T(8,128)(2,...) while((s32[]{:T(128)}, ...), condition=%wide.region_6.9_spmd.clone, body=%wide.region_5.8_spmd.clone.sunk | while | flops 1357005952 | bytes 25215972 | solution.py:148
  125.3 1.6 fusion.114
  126.9 1.5 fusion.117
  128.4 2.5 %fusion.115 = bf16[1,4,256,1024]{2,3,1,0:T(8,128)(2,1)S(1)} fusion(f32[1024,256,4]{1,0,2:T(8,128)S(1)} %fusion.114, f32[4,256]{1,0:T(4,128)S(1)} %bitcast.251, f32[4,256]{1,0:T(4,128)S(1)} %bitcast.253, pred[256,1024]{0,1:T(8,128)(4,1)S(1)} %copy.73, bf16[256,1,4,128]{0,3,2,1:T(8,128)(2,1)S(1)} %get-tuple-element.869, ...), kind=kOutput, calls=%fused_computation.40.clone.1 | convolution fusion | flops 275775488 | bytes 7086084 | tf_op jit(solution)/shard_map/while/body/eval_jaxpr/qghd,kgd->ghqk/dot_general | solution.py:108
  137.7 1.6 fusion.114
  140.9 2.5 %fusion.115 = bf16[1,4,256,1024]{2,3,1,0:T(8,128)(2,1)S(1)} fusion(f32[1024,256,4]{1,0,2:T(8,128)S(1)} %fusion.114, f32[4,256]{1,0:T(4,128)S(1)} %bitcast.251, f32[4,256]{1,0:T(4,128)S(1)} %bitcast.253, pred[256,1024]{0,1:T(8,128)(4,1)S(1)} %copy.73, bf16[256,1,4,128]{0,3,2,1:T(8,128)(2,1)S(1)} %get-tuple-element.869, ...), kind=kOutput, calls=%fused_computation.40.clone.1 | convolution fusion | flops 275775488 | bytes 7086084 | tf_op jit(solution)/shard_map/while/body/eval_jaxpr/qghd,kgd->ghqk/dot_general | solution.py:108
  150.2 1.6 fusion.114
  153.4 2.5 %fusion.115 = bf16[1,4,256,1024]{2,3,1,0:T(8,128)(2,1)S(1)} fusion(f32[1024,256,4]{1,0,2:T(8,128)S(1)} %fusion.114, f32[4,256]{1,0:T(4,128)S(1)} %bitcast.251, f32[4,256]{1,0:T(4,128)S(1)} %bitcast.253, pred[256,1024]{0,1:T(8,128)(4,1)S(1)} %copy.73, bf16[256,1,4,128]{0,3,2,1:T(8,128)(2,1)S(1)} %get-tuple-element.869, ...), kind=kOutput, calls=%fused_computation.40.clone.1 | convolution fusion | flops 275775488 | bytes 7086084 | tf_op jit(solution)/shard_map/while/body/eval_jaxpr/qghd,kgd->ghqk/dot_general | solution.py:108
  162.6 1.6 fusion.114
  165.8 2.5 %fusion.115 = bf16[1,4,256,1024]{2,3,1,0:T(8,128)(2,1)S(1)} fusion(f32[1024,256,4]{1,0,2:T(8,128)S(1)} %fusion.114, f32[4,256]{1,0:T(4,128)S(1)} %bitcast.251, f32[4,256]{1,0:T(4,128)S(1)} %bitcast.253, pred[256,1024]{0,1:T(8,128)(4,1)S(1)} %copy.73, bf16[256,1,4,128]{0,3,2,1:T(8,128)(2,1)S(1)} %get-tuple-element.869, ...), kind=kOutput, calls=%fused_computation.40.clone.1 | convolution fusion | flops 275775488 | bytes 7086084 | tf_op jit(solution)/shard_map/while/body/eval_jaxpr/qghd,kgd->ghqk/dot_general | solution.py:108
  171.4 3.9 %copy.45 = bf16[4,1024,256]{2,1,0:T(8,128)(2,1)} copy(bf16[4,1024,256]{1,2,0:T(8,128)(2,1)} %get-tuple-element.424) | data formatting | bytes 4194304 | tf_op jit(solution)/shard_map/convert_element_type | solution.py:158
  177.2 57.0 %reduce-scatter.2.cloned.1.call-done = bf16[256,256]{1,0:T(8,128)(2,1)} async-done(((bf16[4096,256]{1,0:T(8,128)(2,1)}), bf16[256,256]{1,0:T(8,128)(2,1)}) %reduce-scatter.2.cloned.1.call-update) | async-done | bytes 131088 | tf_op jit(solution)/shard_map/reduce_scatter | solution.py:157
  234.2 1.6 fusion.75
  (151 shorter events, 50.2 us)
Async XLA Ops:
  7.2 2.4 copy-start
  7.2 44.2 %all-gather.3.cloned.1.call-start = ((), (), s32[]{:S(2)}) async-start(), calls=%async_computation.1 | async-start | bytes 1114112 | tf_op jit(solution)/shard_map/all_gather | solution.py:78
  7.9 82.4 %all-gather.5.cloned.1.call-start = ((), (), s32[]{:S(2)}) async-start(), calls=%async_computation.2 | async-start | bytes 1114112 | tf_op jit(solution)/shard_map/all_gather | solution.py:79
  8.7 225.6 %reduce-scatter.2.cloned.1.call-start = ((), (), s32[]{:S(2)}) async-start(), calls=%async_computation.3 | async-start | bytes 2228224 | tf_op jit(solution)/shard_map/reduce_scatter | solution.py:157
Sparse Core Ops, SparseCore 0:
  9.8 41.4 all-gather.2
  53.2 37.0 all-gather.4
  175.5 58.6 reduce-scatter.1
where the time goes:
time: 243 us; the launch traced here: 242 us
  waiting for transfers between devices  136 us (56%)
  matrix products  48.5 us (20%)
  local copies, waits for them, and re-layouts  22.7 us (9%)
  other arithmetic  17.7 us (7%)
  between operations  13.9 us (6%)
  loops' own time  3.33 us (1%)
    reduce_scatter x1, waiting for transfers between devices, per_device(): lax.psum_scatter(key_terms.astype(jnp.bfloat16), 'seq', scatter_dimension...  57 us
    all_gather x1, waiting for transfers between devices, per_device(): value_piece = lax.all_gather(value_rows, 'seq', axis=0, tiled=True)  39 us
    all_gather x1, waiting for transfers between devices, per_device(): key_piece = lax.all_gather(key_rows, 'seq', axis=0, tiled=True)  38.7 us
    dot_general x8, matrix products, masked_scores(): jnp.einsum('qghd,kgd->ghqk', query_heads, key_block, preferred_element_ty...  13.6 us
    dot_general x4, matrix products, backward_block(): jnp.einsum('qghd,kgd->ghqk', grad_heads, value_block, preferred_element_t...  9.81 us
    dot_general x4, matrix products, forward_block(): jnp.einsum('ghqk,kgd->ghqd', softmax_terms.astype(jnp.bfloat16), value_bl...  9.75 us
    dot_general x4, matrix products, backward_block(): jnp.einsum('ghqk,qghd->kgd', softmax_terms.astype(jnp.bfloat16), grad_hea...  6.03 us
    dot_general x4, matrix products, backward_block(): jnp.einsum('ghqk,kgd->qghd', dscores, key_block, preferred_element_type=j...  6.02 us
  transfers between devices with their start and end apart: 3, of which 3 were waited for; matrix products, arithmetic and copies ran while one was open for 2% of the time, Pallas kernels for 0%

commit v1 on v0

v1 whole, which is shorter than its diff:
```python
import jax
import jax.numpy as jnp
from jax import lax
from jax.experimental import pallas as pl
from jax.experimental.pallas import tpu as pltpu
from jax.sharding import PartitionSpec as P

HD = 128
TILE = 128
LOG2E = 1.4426950408889634
FAR_BELOW = -1e30
MESH = pl.DeviceIdType.MESH
VMEM = pl.BlockSpec(memory_space=pltpu.VMEM)
SMEM = pl.BlockSpec(memory_space=pltpu.SMEM)
ANY = pl.BlockSpec(memory_space=pl.ANY)


def places(ring):
    me = lax.axis_index("seq")
    z = me // 2
    core = me % 2
    right = ((z + 1) % ring) * 2 + core
    left = ((z + ring - 1) % ring) * 2 + core
    partner = z * 2 + 1 - core
    return me, z, core, right, left, partner


def meet(right, left, partner):
    barrier = pltpu.get_barrier_semaphore()
    for peer in (right, left, partner):
        pl.semaphore_signal(barrier, inc=1, device_id={"seq": peer}, device_id_type=MESH)
    pl.semaphore_wait(barrier, 3)


def chain_length(direction, chunk, ring):
    long_way = (chunk < 2) == (direction == 0)
    return ring // 2 if long_way else ring - 1 - ring // 2


def gather_kernel(ring, key_ref, value_ref, keys_out, values_out, send_sem, recv_sem, pair_send, pair_recv, own_sem):
    me, z, core, right, left, partner = places(ring)
    meet(right, left, partner)
    peers = (right, left)
    outs = (keys_out, keys_out, values_out, values_out)
    mine = (key_ref, key_ref, value_ref, value_ref)

    def part(chunk, owner):
        return outs[chunk].at[pl.ds(pl.multiple_of(owner * 2 * TILE + (chunk % 2) * TILE, TILE), TILE)]

    def own(chunk):
        return mine[chunk].at[pl.ds((chunk % 2) * TILE, TILE)]

    def owner_at(direction, hop, column):
        step = ring - hop if direction == 0 else hop
        return ((z + step) % ring) * 2 + column

    def hop_copy(direction, hop, chunk):
        owner = owner_at(direction, hop, core)
        source = own(chunk) if hop == 0 else part(chunk, owner)
        return pltpu.make_async_remote_copy(
            src_ref=source, dst_ref=part(chunk, owner),
            send_sem=send_sem.at[direction, hop, chunk], recv_sem=recv_sem.at[direction, hop, chunk],
            device_id={"seq": peers[direction]}, device_id_type=MESH)

    def arrival(direction, hop, chunk):
        owner = owner_at(direction, hop + 1, core)
        return pltpu.make_async_remote_copy(
            src_ref=part(chunk, owner), dst_ref=part(chunk, owner),
            send_sem=send_sem.at[direction, hop, chunk], recv_sem=recv_sem.at[direction, hop, chunk],
            device_id={"seq": peers[direction]}, device_id_type=MESH)

    def pair_copy(slot, chunk, source, owner):
        return pltpu.make_async_remote_copy(
            src_ref=source, dst_ref=part(chunk, owner),
            send_sem=pair_send.at[slot, chunk], recv_sem=pair_recv.at[slot, chunk],
            device_id={"seq": partner}, device_id_type=MESH)

    sent = []
    for chunk in range(4):
        for direction in range(2):
            copy = hop_copy(direction, 0, chunk)
            copy.start()
            sent.append(copy)
    pairs = []
    for chunk in range(4):
        copy = pair_copy(0, chunk, own(chunk), me)
        copy.start()
        pairs.append(copy)
    locals_ = []
    for chunk in range(4):
        copy = pltpu.make_async_copy(own(chunk), part(chunk, me), own_sem.at[chunk])
        copy.start()
        locals_.append(copy)
    for hop in range(ring // 2):
        for chunk in range(4):
            for direction in range(2):
                if hop >= chain_length(direction, chunk, ring):
                    continue
                arrival(direction, hop, chunk).wait_recv()
                if hop + 1 < chain_length(direction, chunk, ring):
                    copy = hop_copy(direction, hop + 1, chunk)
                    copy.start()
                    sent.append(copy)
                owner = owner_at(direction, hop + 1, core)
                slot = hop + 1 if direction == 0 else ring - 1 - hop
                copy = pair_copy(slot, chunk, part(chunk, owner), owner)
                copy.start()
                pairs.append(copy)
    for copy in locals_:
        copy.wait()
    for copy in sent:
        copy.wait_send()
    for slot in range(ring):
        for chunk in range(4):
            owner = owner_at(0, slot, 1 - core)
            pair_copy(slot, chunk, part(chunk, owner), owner).wait_recv()
    for copy in pairs:
        copy.wait_send()


def gather(ring, keys, values):
    rows = keys.shape[0] * ring * 2
    return pl.pallas_call(
        lambda *refs: gather_kernel(ring, *refs),
        out_shape=(jax.ShapeDtypeStruct((rows, HD), jnp.bfloat16),) * 2,
        in_specs=[VMEM, VMEM],
        out_specs=(VMEM, VMEM),
        scratch_shapes=[
            pltpu.SemaphoreType.DMA((2, ring // 2, 4)),
            pltpu.SemaphoreType.DMA((2, ring // 2, 4)),
            pltpu.SemaphoreType.DMA((ring, 4)),
            pltpu.SemaphoreType.DMA((ring, 4)),
            pltpu.SemaphoreType.DMA((4,)),
        ],
        name="gather",
        compiler_params=pltpu.CompilerParams(collective_id=0, has_side_effects=True),
    )(keys, values)


def dot(a, b, a_dim, b_dim):
    return lax.dot_general(a, b, (((a_dim,), (b_dim,)), ((), ())), preferred_element_type=jnp.float32)


def attention_kernel(heads, tiles, ids, mask, q_ref, g_ref, k_ref, v_ref,
                     att_ref, dq_ref, dk_ref, dv_ref,
                     listed, q_rows, g_rows, q_turned, g_turned, total, terms, maxima, dk_acc, dv_acc):
    factor = HD ** -0.5
    wide = heads * TILE
    me = lax.axis_index("seq")
    own_tiles = q_ref.shape[0] // TILE

    dk_acc[...] = jnp.zeros_like(dk_acc)
    dv_acc[...] = jnp.zeros_like(dv_acc)

    for a in range(own_tiles):
        rows = pl.ds(a * TILE, TILE)
        place = me * own_tiles + a
        query_tile = ids[place]
        listed[0] = place

        def build(j, n):
            ok = jnp.logical_and(mask[query_tile, ids[j]] == 1, j != place)
            listed[n] = j
            return n + ok.astype(jnp.int32)

        count = lax.fori_loop(0, tiles, build, jnp.int32(1))
        listed[count] = place
        steps = (count + 1) // 2

        for h in range(heads):
            column = pl.ds(h * HD, HD)
            block = pl.ds(h * TILE, TILE)
            q_block = q_ref[rows, column]
            g_block = g_ref[rows, column]
            q_rows[block, :] = q_block
            g_rows[block, :] = g_block
            q_turned[:, block] = q_block.T
            g_turned[:, block] = g_block.T

        def pair_of(ref, s):
            first = pl.ds(pl.multiple_of(listed[2 * s] * TILE, TILE), TILE)
            second = pl.ds(pl.multiple_of(listed[2 * s + 1] * TILE, TILE), TILE)
            return jnp.concatenate([ref[first, :], ref[second, :]], axis=0)

        def scores_of(s):
            scores = dot(pair_of(k_ref, s), q_turned[...], 1, 0) * (factor * LOG2E)
            bias = jnp.where(2 * s + 1 < count, 0.0, FAR_BELOW)
            return scores[:TILE], scores[TILE:] + bias

        def keep(s, upper, lower, top):
            upper = jnp.exp2(upper - top)
            lower = jnp.exp2(lower - top)
            both = jnp.concatenate([upper, lower], axis=0)
            terms[s] = both
            maxima[s] = top
            return jnp.sum(both, axis=0, keepdims=True), dot(pair_of(v_ref, s), both.astype(jnp.bfloat16), 0, 0)

        upper, lower = scores_of(0)
        key_place = lax.broadcasted_iota(jnp.int32, (TILE, wide), 0)
        query_place = lax.broadcasted_iota(jnp.int32, (TILE, wide), 1) % TILE
        upper = jnp.where(query_place >= key_place, upper, FAR_BELOW)
        top = jnp.max(jnp.maximum(upper, lower), axis=0, keepdims=True)
        share, weighted = keep(0, upper, lower, top)
        total[...] = weighted

        def forward(s, carried):
            top, share = carried
            upper, lower = scores_of(s)
            new_top = jnp.maximum(top, jnp.max(jnp.maximum(upper, lower), axis=0, keepdims=True))
            shrink = jnp.exp2(top - new_top)
            more, weighted = keep(s, upper, lower, new_top)
            total[...] = total[...] * shrink + weighted
            return new_top, share * shrink + more

        top, share = lax.fori_loop(1, steps, forward, (top, share))
        attended = (total[...] / share).astype(jnp.bfloat16)
        delta = jnp.sum(g_turned[...].astype(jnp.float32) * attended.astype(jnp.float32), axis=0, keepdims=True)
        log_total = top + jnp.log2(share)
        for h in range(heads):
            att_ref[rows, pl.ds(h * HD, HD)] = attended[:, h * TILE:(h + 1) * TILE].T

        total[...] = jnp.zeros_like(total)

        def backward(s, carried):
            probs = terms[s] * jnp.exp2(maxima[s] - log_total)
            dprobs = dot(pair_of(v_ref, s), g_turned[...], 1, 0)
            dscores = (probs * (dprobs - delta)).astype(jnp.bfloat16)
            dv_part = dot(probs.astype(jnp.bfloat16), g_rows[...], 1, 0)
            dk_part = dot(dscores, q_rows[...], 1, 0)
            first = pl.ds(pl.multiple_of(listed[2 * s] * TILE, TILE), TILE)
            second = pl.ds(pl.multiple_of(listed[2 * s + 1] * TILE, TILE), TILE)
            dv_acc[first, :] += dv_part[:TILE]
            dv_acc[second, :] += dv_part[TILE:]
            dk_acc[first, :] += dk_part[:TILE]
            dk_acc[second, :] += dk_part[TILE:]
            total[...] += dot(pair_of(k_ref, s), dscores, 0, 0)
            return carried

        lax.fori_loop(0, steps, backward, jnp.int32(0))
        for h in range(heads):
            dq_ref[rows, pl.ds(h * HD, HD)] = (total[:, h * TILE:(h + 1) * TILE] * factor).T

    dk_ref[...] = (dk_acc[...] * factor).astype(jnp.bfloat16)
    dv_ref[...] = dv_acc[...].astype(jnp.bfloat16)


def attention(queries, grads, keys, values, ids, mask):
    rows, width = queries.shape
    heads = width // HD
    key_total = keys.shape[0]
    tiles = key_total // TILE
    wide = heads * TILE
    return pl.pallas_call(
        lambda *refs: attention_kernel(heads, tiles, *refs),
        out_shape=(
            jax.ShapeDtypeStruct((rows, width), jnp.bfloat16),
            jax.ShapeDtypeStruct((rows, width), jnp.float32),
            jax.ShapeDtypeStruct((key_total, HD), jnp.bfloat16),
            jax.ShapeDtypeStruct((key_total, HD), jnp.bfloat16),
        ),
        in_specs=[SMEM, SMEM, VMEM, VMEM, VMEM, VMEM],
        out_specs=(VMEM,) * 4,
        scratch_shapes=[
            pltpu.SMEM((tiles + 8,), jnp.int32),
            pltpu.VMEM((wide, HD), jnp.bfloat16),
            pltpu.VMEM((wide, HD), jnp.bfloat16),
            pltpu.VMEM((HD, wide), jnp.bfloat16),
            pltpu.VMEM((HD, wide), jnp.bfloat16),
            pltpu.VMEM((HD, wide), jnp.float32),
            pltpu.VMEM((tiles // 2, 2 * TILE, wide), jnp.float32),
            pltpu.VMEM((tiles // 2, 1, wide), jnp.float32),
            pltpu.VMEM((key_total, HD), jnp.float32),
            pltpu.VMEM((key_total, HD), jnp.float32),
        ],
        name="attention",
    )(ids, mask, queries, grads, keys, values)


def scatter_kernel(ring, dk_ref, dv_ref, dk_out, dv_out, landed, outgoing, pair_in,
                   send_sem, recv_sem, pair_send, pair_recv):
    me, z, core, right, left, partner = places(ring)
    meet(right, left, partner)
    peers = (right, left)
    sources = (dk_ref, dk_ref, dv_ref, dv_ref)

    def rows_of(chunk, owner):
        return pl.ds(pl.multiple_of(owner * 2 * TILE + (chunk % 2) * TILE, TILE), TILE)

    def pair_copy(slot, chunk):
        chip = (z + slot) % ring
        return pltpu.make_async_remote_copy(
            src_ref=sources[chunk].at[rows_of(chunk, chip * 2 + 1 - core)], dst_ref=pair_in.at[slot, chunk],
            send_sem=pair_send.at[slot, chunk], recv_sem=pair_recv.at[slot, chunk],
            device_id={"seq": partner}, device_id_type=MESH)

    def ring_copy(direction, hop, chunk):
        return pltpu.make_async_remote_copy(
            src_ref=outgoing.at[direction, hop, chunk], dst_ref=landed.at[direction, hop, chunk],
            send_sem=send_sem.at[direction, hop, chunk], recv_sem=recv_sem.at[direction, hop, chunk],
            device_id={"seq": peers[direction]}, device_id_type=MESH)

    order = []
    for hop in range(ring // 2):
        for chunk in range(4):
            for direction in range(2):
                length = chain_length(direction, chunk, ring)
                if hop < length:
                    away = length - hop
                    order.append((away if direction == 0 else ring - away, chunk))
    order += [(0, chunk) for chunk in range(4)]
    seen = []
    for item in order:
        if item not in seen:
            seen.append(item)
    pairs = []
    for slot, chunk in seen:
        copy = pair_copy(slot, chunk)
        copy.start()
        pairs.append(copy)

    def local_sum(slot, chunk):
        pair_copy(slot, chunk).wait_recv()
        chip = (z + slot) % ring
        return (sources[chunk][rows_of(chunk, chip * 2 + core), :].astype(jnp.float32)
                + pair_in[slot, chunk].astype(jnp.float32))

    sent = []
    ends = {}
    for hop in range(ring // 2):
        for chunk in range(4):
            for direction in range(2):
                length = chain_length(direction, chunk, ring)
                if hop >= length:
                    continue
                away = length - hop
                value = local_sum(away if direction == 0 else ring - away, chunk)
                if hop > 0:
                    ring_copy(direction, hop - 1, chunk).wait_recv()
                    value = value + landed[direction, hop - 1, chunk].astype(jnp.float32)
                outgoing[direction, hop, chunk] = value.astype(jnp.bfloat16)
                copy = ring_copy(direction, hop, chunk)
                copy.start()
                sent.append(copy)
    for chunk in range(4):
        value = local_sum(0, chunk)
        for direction in (0, 1):
            last = chain_length(direction, chunk, ring) - 1
            ring_copy(direction, last, chunk).wait_recv()
            value = value + landed[direction, last, chunk].astype(jnp.float32)
        out = dk_out if chunk < 2 else dv_out
        out[pl.ds((chunk % 2) * TILE, TILE), :] = value
    for copy in sent:
        copy.wait_send()
    for copy in pairs:
        copy.wait_send()


def scatter(ring, dk, dv):
    rows = dk.shape[0] // (2 * ring)
    hops = ring // 2
    return pl.pallas_call(
        lambda *refs: scatter_kernel(ring, *refs),
        out_shape=(jax.ShapeDtypeStruct((rows, HD), jnp.float32),) * 2,
        in_specs=[VMEM, VMEM],
        out_specs=(VMEM, VMEM),
        scratch_shapes=[
            pltpu.VMEM((2, hops, 4, TILE, HD), jnp.bfloat16),
            pltpu.VMEM((2, hops, 4, TILE, HD), jnp.bfloat16),
            pltpu.VMEM((ring, 4, TILE, HD), jnp.bfloat16),
            pltpu.SemaphoreType.DMA((2, hops, 4)),
            pltpu.SemaphoreType.DMA((2, hops, 4)),
            pltpu.SemaphoreType.DMA((ring, 4)),
            pltpu.SemaphoreType.DMA((ring, 4)),
        ],
        name="scatter",
        compiler_params=pltpu.CompilerParams(collective_id=1, has_side_effects=True),
    )(dk, dv)


def solution(mesh):
    ring = mesh.shape["seq"] // 2

    def per_device(queries, key_rows, value_rows, out_grad, tile_ids, tile_mask):
        keys, values = gather(ring, key_rows, value_rows)
        attended, query_grad, dk, dv = attention(queries, out_grad, keys, values, tile_ids, tile_mask)
        key_grad, value_grad = scatter(ring, dk, dv)
        return attended, query_grad, key_grad, value_grad

    spec = P(("batch", "seq"), "head")
    return jax.shard_map(
        per_device,
        mesh=mesh,
        in_specs=(spec, spec, spec, spec, P("batch"), P("batch", None)),
        out_specs=(spec,) * 4,
        check_vma=False,
    )
```

time: 243 us -> 61.2 us (0.25)
  waiting for transfers between devices: 136 us -> 0 us
  Pallas kernels: 0 us -> 57.8 us
  matrix products: 48.5 us -> 0 us
  local copies, waits for them, and re-layouts: 22.7 us -> 2.26 us
  other arithmetic: 17.7 us -> 0 us
  between operations: 13.9 us -> 0.66 us
  loops' own time: 3.33 us -> 0 us
    all_gather x2 -> x0, waiting for transfers between devices: 77.7 us -> none  [the longest x1 39 us: per_device(): value_piece = lax.all_gather(value_rows, 'seq', axis=0, tiled=True)]
    pallas_call x0 -> x3, Pallas kernels: none -> 57.8 us  [the longest x1 24.8 us: gather(): pl.pallas_call(lambda *refs: gather_kernel(ring, *refs), out_shape=(jax.S...]
    reduce_scatter x1 -> x0, waiting for transfers between devices: 57 us -> none  [per_device(): lax.psum_scatter(key_terms.astype(jnp.bfloat16), 'seq', scatter_dimension...]
    dot_general x28 -> x0, matrix products: 48.5 us -> none  [the longest x8 13.6 us: masked_scores(): jnp.einsum('qghd,kgd->ghqk', query_heads, key_block, preferred_element_ty...]
    and x17 -> x0, other arithmetic: 8.48 us -> none  [the longest x8 5.9 us: tile_allowed(): jnp.take(jnp.take(tile_mask, query_tiles, axis=0), key_tiles, axis=1) == 1]
    gather x9 -> x0, local copies, waits for them, and re-layouts: 4.99 us -> none  [the longest x8 4.43 us: tile_allowed(): jnp.take(jnp.take(tile_mask, query_tiles, axis=0), key_tiles, axis=1) == 1]
    convert_element_type x2 -> x0, local copies, waits for them, and re-layouts: 4.78 us -> none  [the longest x1 3.93 us: per_device(): key_terms.astype(jnp.bfloat16)]
    reduce_sum x5 -> x0, other arithmetic: 4.29 us -> none  [the longest x4 4.17 us: forward_block(): denominator = denominator * shrink + jnp.sum(softmax_terms, axis=-1)]
  transfers between devices with their start and end apart: 3 -> 0, of which waited for: 3 -> 0; matrix products, arithmetic and copies ran while one was open for 2% -> 0% of each run, Pallas kernels for 0% -> 0%
where the time goes in v1:
time: 61.2 us; the launch traced here: 60.7 us
  Pallas kernels  57.8 us (94%)
  local copies, waits for them, and re-layouts  2.26 us (4%)
  between operations  0.66 us (1%)
    pallas_call x1, Pallas kernels, gather(): pl.pallas_call(lambda *refs: gather_kernel(ring, *refs), out_shape=(jax.S...  24.8 us
    pallas_call x1, Pallas kernels, scatter(): pl.pallas_call(lambda *refs: scatter_kernel(ring, *refs), out_shape=(jax....  22.8 us
    pallas_call x1, Pallas kernels, attention(): pl.pallas_call(lambda *refs: attention_kernel(heads, tiles, *refs), out_s...  10.2 us
    unnamed x4, local copies, waits for them, and re-layouts  2.26 us

profile of v1, /device:TPU:2, one launch (start us, length us, event | category | flops | bytes accessed | tf_op | source)
XLA Modules:
  0.0 60.7 jit_solution(10754046930306755460)
XLA Ops:
  0.6 24.8 %gather.1 = (bf16[4096,128]{1,0:T(8,128)(2,1)}, bf16[4096,128]{1,0:T(8,128)(2,1)}) custom-call(bf16[256,128]{1,0:T(8,128)(2,1)} %refs_0_.2, bf16[256,128]{1,0:T(8,128)(2,1)} %refs_1_.2), custom_call_target="tpu_custom_call" | custom-call | tf_op jit(solution)/shard_map/gather/pallas_call | solution.py:123
  25.4 10.2 %attention.1 = (bf16[256,512]{1,0:T(8,128)(2,1)}, f32[256,512]{1,0:T(8,128)}, bf16[4096,128]{1,0:T(8,128)(2,1)}, bf16[4096,128]{1,0:T(8,128)(2,1)}) custom-call(s32[32]{0:T(128)} %refs_0_.3, s32[32,32]{1,0:T(8,128)} %refs_1_.3, bf16[256,512]{1,0:T(8,128)(2,1)} %refs_2_.1, bf16[256,512]{1,0:T(8,128)(2,1)} %refs_3_.1, ...), custom_call_target="tpu_custom_call" | custom-call | tf_op jit(solution)/shard_map/attention/pallas_call | solution.py:253
  35.7 22.8 %scatter.1 = (f32[256,128]{1,0:T(8,128)}, f32[256,128]{1,0:T(8,128)}) custom-call(bf16[4096,128]{1,0:T(8,128)(2,1)} %get-tuple-element.16.refs_0_, bf16[4096,128]{1,0:T(8,128)(2,1)} %get-tuple-element.17.refs_1_), custom_call_target="tpu_custom_call" | custom-call | tf_op jit(solution)/shard_map/scatter/pallas_call | solution.py:361
  58.4 0.0 copy-start
  58.5 1.6 %copy.12 = f32[256,128]{1,0:T(8,128)} copy(f32[256,128]{1,0:T(8,128)} %get-tuple-element.26) | data formatting | bytes 262144
  60.1 0.0 copy-done
  60.1 0.7 %copy.13 = f32[256,128]{1,0:T(8,128)} copy(f32[256,128]{1,0:T(8,128)S(1)} %copy-done) | data formatting | bytes 262144
Async XLA Ops:
  58.4 1.6 %copy-start = (f32[256,128]{1,0:T(8,128)S(1)}, f32[256,128]{1,0:T(8,128)}, u32[]{:S(2)}) copy-start(f32[256,128]{1,0:T(8,128)} %get-tuple-element.27) | copy-start | bytes 393220

commit v2 on v0

v2 whole, which is shorter than its diff:
```python
import jax
import jax.numpy as jnp
from jax import lax
from jax.experimental import pallas as pl
from jax.experimental.pallas import tpu as pltpu
from jax.sharding import PartitionSpec as P

HD = 128
TILE = 128
BLOCK = 2 * TILE
LOG2E = 1.4426950408889634
FAR_BELOW = -1e30
MESH = pl.DeviceIdType.MESH
VMEM = pl.BlockSpec(memory_space=pltpu.VMEM)
SMEM = pl.BlockSpec(memory_space=pltpu.SMEM)
RING = 8


def dot(a, b):
    return lax.dot_general(a, b, (((1,), (0,)), ((), ())), preferred_element_type=jnp.float32)


def kernel(heads, ids, mask, q_ref, g_ref, k_ref, v_ref, att_ref, dq_ref, dk_ref, dv_ref,
           kv, q_rows, g_rows, q_turned, g_turned, bias, terms, maxima, total, top_ref, share_ref, delta_ref,
           own_part, pair_out, pair_in, outgoing, landed,
           gather_send, gather_recv, share_send, share_recv, pair_send, pair_recv, ring_send, ring_recv):
    factor = HD ** -0.5
    wide = 2 * heads * TILE
    columns = [slice(n * BLOCK, (n + 1) * BLOCK) for n in range(wide // BLOCK)]
    blocks_per_tile = len(columns) // 2
    me = lax.axis_index("seq")
    z = me // 2
    core = me % 2
    peers = (((z + 1) % RING) * 2 + core, ((z + RING - 1) % RING) * 2 + core)
    partner = z * 2 + 1 - core

    barrier = pltpu.get_barrier_semaphore()
    for peer in peers + (partner,):
        pl.semaphore_signal(barrier, inc=1, device_id={"seq": peer}, device_id_type=MESH)
    pl.semaphore_wait(barrier, 3)

    def own_chunk(chunk):
        return (k_ref if chunk < 2 else v_ref).at[pl.ds((chunk % 2) * TILE, TILE)]

    def hop_copy(direction, hop, chunk, source=None):
        offset = RING - hop if direction == 0 else hop
        place = kv.at[((z + offset) % RING) * 2 + core, chunk]
        return pltpu.make_async_remote_copy(
            src_ref=place if source is None else source, dst_ref=place,
            send_sem=gather_send.at[direction, hop, chunk], recv_sem=gather_recv.at[direction, hop, chunk],
            device_id={"seq": peers[direction]}, device_id_type=MESH)

    def share_copy(back, chunk, column, source=None):
        place = kv.at[((z + RING - back) % RING) * 2 + column, chunk]
        return pltpu.make_async_remote_copy(
            src_ref=place if source is None else source, dst_ref=place,
            send_sem=share_send.at[back, chunk], recv_sem=share_recv.at[back, chunk],
            device_id={"seq": partner}, device_id_type=MESH)

    for n in range(4):
        for direction in range(2):
            chunk = (n + 2 * direction) % 4
            hop_copy(direction, 0, chunk, own_chunk(chunk)).start()
    for chunk in range(4):
        share_copy(0, chunk, core, own_chunk(chunk)).start()
    for r in range(2):
        kv[me, r] = k_ref[pl.ds(r * TILE, TILE), :]
        kv[me, 2 + r] = v_ref[pl.ds(r * TILE, TILE), :]

    def gather_slot(j):
        hop = j // 4
        for direction in range(2):
            chunk = (j + 2 * direction) % 4
            offset = RING - hop - 1 if direction == 0 else hop + 1
            place = kv.at[((z + offset) % RING) * 2 + core, chunk]
            pltpu.make_async_remote_copy(
                src_ref=place, dst_ref=place,
                send_sem=gather_send.at[direction, hop, chunk], recv_sem=gather_recv.at[direction, hop, chunk],
                device_id={"seq": peers[direction]}, device_id_type=MESH).wait_recv()

            @pl.when(j < 10)
            def _():
                hop_copy(direction, hop + 1, chunk).start()

            share_copy((RING - offset) % RING, chunk, core).start()

    row = lax.broadcasted_iota(jnp.int32, (TILE, TILE), 0)
    lane = lax.broadcasted_iota(jnp.int32, (TILE, TILE), 1)
    bias[0] = jnp.zeros((TILE, TILE), jnp.float32)
    bias[1] = jnp.where(lane >= row, 0.0, FAR_BELOW)
    bias[2] = jnp.full((TILE, TILE), FAR_BELOW, jnp.float32)
    for a in range(2):
        for h in range(heads):
            block = pl.ds((a * heads + h) * TILE, TILE)
            q_block = q_ref[pl.ds(a * TILE, TILE), pl.ds(h * HD, HD)]
            g_block = g_ref[pl.ds(a * TILE, TILE), pl.ds(h * HD, HD)]
            q_rows[block, :] = q_block
            g_rows[block, :] = g_block
            q_turned[:, block] = q_block.T
            g_turned[:, block] = g_block.T
    top_ref[...] = jnp.full_like(top_ref, FAR_BELOW)
    share_ref[...] = jnp.zeros_like(share_ref)
    total[...] = jnp.zeros_like(total)

    def bias_block(owner, r, a):
        state = jnp.where(mask[ids[me * 2 + a], ids[owner * 2 + r]] == 1, 0, 2)
        state = jnp.where(owner * 2 + r == me * 2 + a, 1, state)
        one = bias[state]
        return jnp.concatenate([one] * (BLOCK // TILE), axis=1)

    def forward_unit(owner):
        keys = kv[owner, 0:2].reshape(BLOCK, HD)
        values_turned = kv[owner, 2:4].reshape(BLOCK, HD).T
        biases = [jnp.concatenate([bias_block(owner, 0, a), bias_block(owner, 1, a)], axis=0) for a in range(2)]
        for n, column in enumerate(columns):
            scores = dot(keys, q_turned[:, column]) * (factor * LOG2E) + biases[n // blocks_per_tile]
            old = top_ref[:, column]
            top = jnp.maximum(old, jnp.max(scores, axis=0, keepdims=True))
            shrink = jnp.exp2(old - top)
            probs = jnp.exp2(scores - top)
            terms[owner, :, column] = probs
            maxima[owner, :, column] = top
            top_ref[:, column] = top
            share_ref[:, column] = share_ref[:, column] * shrink + jnp.sum(probs, axis=0, keepdims=True)
            total[:, column] = total[:, column] * shrink + dot(values_turned, probs.astype(jnp.bfloat16))

    def forward_step(j, carried):
        unit = jnp.where(j < 2, j, j - 2)

        @pl.when(jnp.logical_or(j < 2, j >= 4))
        def _():
            rest = jnp.maximum(unit - 2, 0)
            near = rest // 4
            which = rest % 4
            back = jnp.where(which % 2 == 0, near + 1, RING - 1 - near)
            other = jnp.where(near == 3, which, which // 2)
            back = jnp.where(unit < 2, 0, back)
            other = jnp.where(unit < 2, unit, other)
            column = jnp.where(other == 1, 1 - core, core)

            @pl.when(other == 1)
            def _():
                for chunk in range(4):
                    share_copy(back, chunk, 1 - core).wait_recv()

            forward_unit(((z + RING - back) % RING) * 2 + column)

        @pl.when(j < 14)
        def _():
            gather_slot(j)

        return carried

    lax.fori_loop(0, 18, forward_step, 0)

    attended = (total[...] / share_ref[...]).astype(jnp.bfloat16)
    delta_ref[...] = jnp.sum(g_turned[...].astype(jnp.float32) * attended.astype(jnp.float32), axis=0, keepdims=True)
    top_ref[...] = top_ref[...] + jnp.log2(share_ref[...])
    for a in range(2):
        for h in range(heads):
            n = a * heads + h
            att_ref[pl.ds(a * TILE, TILE), pl.ds(h * HD, HD)] = attended[:, n * TILE:(n + 1) * TILE].T
    total[...] = jnp.zeros_like(total)

    def pair_copy(n):
        return pltpu.make_async_remote_copy(
            src_ref=pair_out.at[n], dst_ref=pair_in.at[n], send_sem=pair_send.at[n], recv_sem=pair_recv.at[n],
            device_id={"seq": partner}, device_id_type=MESH)

    def ring_copy(direction, hop, which):
        return pltpu.make_async_remote_copy(
            src_ref=outgoing.at[direction, hop, which], dst_ref=landed.at[direction, hop, which],
            send_sem=ring_send.at[direction, hop, which], recv_sem=ring_recv.at[direction, hop, which],
            device_id={"seq": peers[direction]}, device_id_type=MESH)

    def pass_on(direction, hop, which, n):
        value = own_part[n, which] + pair_in[n, which].astype(jnp.float32)
        outgoing[direction, hop, which] = value.astype(jnp.bfloat16)

        @pl.when(hop > 0)
        def _():
            before = jnp.maximum(hop - 1, 0)
            ring_copy(direction, before, which).wait_recv()
            outgoing[direction, hop, which] = (value + landed[direction, before, which].astype(jnp.float32)).astype(jnp.bfloat16)

        ring_copy(direction, hop, which).start()

    def backward_unit(owner):
        keys_turned = kv[owner, 0:2].reshape(BLOCK, HD).T
        values = kv[owner, 2:4].reshape(BLOCK, HD)
        probs_all, dscores_all = [], []
        for n, column in enumerate(columns):
            probs = terms[owner, :, column] * jnp.exp2(maxima[owner, :, column] - top_ref[:, column])
            dprobs = dot(values, g_turned[:, column])
            dscores = (probs * (dprobs - delta_ref[:, column])).astype(jnp.bfloat16)
            probs_all.append(probs.astype(jnp.bfloat16))
            dscores_all.append(dscores)
            total[:, column] += dot(keys_turned, dscores)
        dk = dot(jnp.concatenate(dscores_all, axis=1), q_rows[...]) * factor
        dv = dot(jnp.concatenate(probs_all, axis=1), g_rows[...])
        return dk, dv

    def backward_step(i, carried):
        n = i // 2
        back = jnp.where(n % 2 == 1, RING - (7 - n) // 2, (8 - n) // 2) % RING
        column = jnp.where(i % 2 == 0, 1 - core, core)
        dk, dv = backward_unit(((z + RING - back) % RING) * 2 + column)

        @pl.when(i % 2 == 0)
        def _():
            pair_out[n, 0] = dk.astype(jnp.bfloat16)
            pair_out[n, 1] = dv.astype(jnp.bfloat16)
            pair_copy(n).start()

        @pl.when(i % 2 == 1)
        def _():
            own_part[n, 0] = dk
            own_part[n, 1] = dv

        @pl.when(i % 4 == 2)
        def _():
            burst = i // 4

            @pl.when(burst == 0)
            def _():
                pair_copy(0).wait_recv()

            @pl.when(burst > 0)
            def _():
                pair_copy(2 * burst - 1).wait_recv()
                pair_copy(2 * burst).wait_recv()

            right = jnp.maximum(2 * burst - 1, 0)
            pass_on(0, burst, 0, right)
            pass_on(1, burst, 1, 2 * burst)

            @pl.when(burst > 0)
            def _():
                pass_on(0, jnp.maximum(burst - 1, 0), 1, right)
                pass_on(1, jnp.maximum(burst - 1, 0), 0, 2 * burst)

        return carried

    lax.fori_loop(0, 16, backward_step, 0)

    for a in range(2):
        for h in range(heads):
            n = a * heads + h
            dq_ref[pl.ds(a * TILE, TILE), pl.ds(h * HD, HD)] = (total[:, n * TILE:(n + 1) * TILE] * factor).T

    pair_copy(7).wait_recv()
    for which, out in ((1, dv_ref), (0, dk_ref)):
        value = own_part[7, which] + pair_in[7, which].astype(jnp.float32)
        for direction in range(2):
            last = 3 if which == direction else 2
            ring_copy(direction, last, which).wait_recv()
            value = value + landed[direction, last, which].astype(jnp.float32)
        out[...] = value

    for direction in range(2):
        for hop in range(4):
            for chunk in range(4):
                if hop < 3 or (chunk < 2) == (direction == 0):
                    hop_copy(direction, hop, chunk).wait_send()
            for which in range(2):
                if hop < 3 or which == direction:
                    ring_copy(direction, hop, which).wait_send()
    for back in range(RING):
        pair_copy(back).wait_send()
        for chunk in range(4):
            share_copy(back, chunk, core).wait_send()


def fused(queries, grads, keys, values, ids, mask):
    rows, width = queries.shape
    heads = width // HD
    devices = 2 * RING
    wide = 2 * heads * TILE
    f32, bf16 = jnp.float32, jnp.bfloat16
    dma = pltpu.SemaphoreType.DMA
    return pl.pallas_call(
        lambda *refs: kernel(heads, *refs),
        out_shape=(
            jax.ShapeDtypeStruct((rows, width), bf16),
            jax.ShapeDtypeStruct((rows, width), f32),
            jax.ShapeDtypeStruct((rows, HD), f32),
            jax.ShapeDtypeStruct((rows, HD), f32),
        ),
        in_specs=[SMEM, SMEM, VMEM, VMEM, VMEM, VMEM],
        out_specs=(VMEM,) * 4,
        scratch_shapes=[
            pltpu.VMEM((devices, 4, TILE, HD), bf16),
            pltpu.VMEM((wide, HD), bf16),
            pltpu.VMEM((wide, HD), bf16),
            pltpu.VMEM((HD, wide), bf16),
            pltpu.VMEM((HD, wide), bf16),
            pltpu.VMEM((3, TILE, TILE), f32),
            pltpu.VMEM((devices, BLOCK, wide), f32),
            pltpu.VMEM((devices, 1, wide), f32),
            pltpu.VMEM((HD, wide), f32),
            pltpu.VMEM((1, wide), f32),
            pltpu.VMEM((1, wide), f32),
            pltpu.VMEM((1, wide), f32),
            pltpu.VMEM((RING, 2, BLOCK, HD), f32),
            pltpu.VMEM((RING, 2, BLOCK, HD), bf16),
            pltpu.VMEM((RING, 2, BLOCK, HD), bf16),
            pltpu.VMEM((2, 4, 2, BLOCK, HD), bf16),
            pltpu.VMEM((2, 4, 2, BLOCK, HD), bf16),
            dma((2, 4, 4)),
            dma((2, 4, 4)),
            dma((RING, 4)),
            dma((RING, 4)),
            dma((RING,)),
            dma((RING,)),
            dma((2, 4, 2)),
            dma((2, 4, 2)),
        ],
        name="fused",
        compiler_params=pltpu.CompilerParams(collective_id=0, has_side_effects=True),
    )(ids, mask, queries, grads, keys, values)


def solution(mesh):
    def per_device(queries, key_rows, value_rows, out_grad, tile_ids, tile_mask):
        return fused(queries, out_grad, key_rows, value_rows, tile_ids, tile_mask)

    spec = P(("batch", "seq"), "head")
    return jax.shard_map(
        per_device,
        mesh=mesh,
        in_specs=(spec, spec, spec, spec, P("batch"), P("batch", None)),
        out_specs=(spec,) * 4,
        check_vma=False,
    )
```

time: 243 us -> 63.8 us (0.26)
  waiting for transfers between devices: 136 us -> 0 us
  Pallas kernels: 0 us -> 58.6 us
  matrix products: 48.5 us -> 0 us
  local copies, waits for them, and re-layouts: 22.7 us -> 4.36 us
  other arithmetic: 17.7 us -> 0 us
  between operations: 13.9 us -> 0.65 us
  loops' own time: 3.33 us -> 0 us
    all_gather x2 -> x0, waiting for transfers between devices: 77.7 us -> none  [the longest x1 39 us: per_device(): value_piece = lax.all_gather(value_rows, 'seq', axis=0, tiled=True)]
    pallas_call x0 -> x1, Pallas kernels: none -> 58.6 us  [fused(): pl.pallas_call(lambda *refs: kernel(heads, *refs), out_shape=(jax.ShapeDt...]
    reduce_scatter x1 -> x0, waiting for transfers between devices: 57 us -> none  [per_device(): lax.psum_scatter(key_terms.astype(jnp.bfloat16), 'seq', scatter_dimension...]
    dot_general x28 -> x0, matrix products: 48.5 us -> none  [the longest x8 13.6 us: masked_scores(): jnp.einsum('qghd,kgd->ghqk', query_heads, key_block, preferred_element_ty...]
    and x17 -> x0, other arithmetic: 8.48 us -> none  [the longest x8 5.9 us: tile_allowed(): jnp.take(jnp.take(tile_mask, query_tiles, axis=0), key_tiles, axis=1) == 1]
    gather x9 -> x0, local copies, waits for them, and re-layouts: 4.99 us -> none  [the longest x8 4.43 us: tile_allowed(): jnp.take(jnp.take(tile_mask, query_tiles, axis=0), key_tiles, axis=1) == 1]
    convert_element_type x2 -> x0, local copies, waits for them, and re-layouts: 4.78 us -> none  [the longest x1 3.93 us: per_device(): key_terms.astype(jnp.bfloat16)]
    reduce_sum x5 -> x0, other arithmetic: 4.29 us -> none  [the longest x4 4.17 us: forward_block(): denominator = denominator * shrink + jnp.sum(softmax_terms, axis=-1)]
  transfers between devices with their start and end apart: 3 -> 0, of which waited for: 3 -> 0; matrix products, arithmetic and copies ran while one was open for 2% -> 0% of each run, Pallas kernels for 0% -> 0%
where the time goes in v2:
time: 63.8 us; the launch traced here: 63.6 us
  Pallas kernels  58.6 us (92%)
  local copies, waits for them, and re-layouts  4.36 us (7%)
  between operations  0.65 us (1%)
    pallas_call x1, Pallas kernels, fused(): pl.pallas_call(lambda *refs: kernel(heads, *refs), out_shape=(jax.ShapeDt...  58.6 us
    unnamed x10, local copies, waits for them, and re-layouts  4.36 us

profile of v2, /device:TPU:2, one launch (start us, length us, event | category | flops | bytes accessed | tf_op | source)
XLA Modules:
  0.0 63.6 jit_solution(17679042672975955713)
XLA Ops:
  0.6 58.6 %fused.1 = (bf16[256,512]{1,0:T(8,128)(2,1)}, f32[256,512]{1,0:T(8,128)}, f32[256,128]{1,0:T(8,128)}, f32[256,128]{1,0:T(8,128)}) custom-call(s32[32]{0:T(128)} %refs_0_.1, s32[32,32]{1,0:T(8,128)} %refs_1_.1, bf16[256,512]{1,0:T(8,128)(2,1)} %refs_2_.1, bf16[256,512]{1,0:T(8,128)(2,1)} %refs_3_.1, bf16[256,128]{1,0:T(8,128)(2,1)} %refs_4_.1, ...), custom_call_target="tpu_custom_call" | custom-call | tf_op jit(solution)/shard_map/fused/pallas_call | solution.py:281
  59.2 0.0 copy-start
  59.2 1.7 %copy.14 = bf16[256,512]{1,0:T(8,128)(2,1)} copy(bf16[256,512]{1,0:T(8,128)(2,1)} %get-tuple-element.8) | data formatting | bytes 524288
  61.0 0.0 copy-done
  61.0 0.0 copy-start.2
  61.0 0.8 %copy.15 = f32[256,512]{1,0:T(8,128)} copy(f32[256,512]{1,0:T(8,128)S(1)} %copy-done) | data formatting | bytes 1048576
  61.8 0.2 copy-done.2
  62.0 0.0 copy-start.1
  62.0 0.7 %copy.16 = f32[256,128]{1,0:T(8,128)} copy(f32[256,128]{1,0:T(8,128)S(1)} %copy-done.2) | data formatting | bytes 262144
  62.7 0.3 copy-done.1
  62.9 0.7 %copy.17 = f32[256,128]{1,0:T(8,128)} copy(f32[256,128]{1,0:T(8,128)S(1)} %copy-done.1) | data formatting | bytes 262144
Async XLA Ops:
  59.2 1.7 %copy-start = (f32[256,512]{1,0:T(8,128)S(1)}, f32[256,512]{1,0:T(8,128)}, u32[]{:S(2)}) copy-start(f32[256,512]{1,0:T(8,128)} %get-tuple-element.9) | copy-start | bytes 1572868
  61.0 1.0 %copy-start.2 = (f32[256,128]{1,0:T(8,128)S(1)}, f32[256,128]{1,0:T(8,128)}, u32[]{:S(2)}) copy-start(f32[256,128]{1,0:T(8,128)} %get-tuple-element.10) | copy-start | bytes 393220
  62.0 1.0 %copy-start.1 = (f32[256,128]{1,0:T(8,128)S(1)}, f32[256,128]{1,0:T(8,128)}, u32[]{:S(2)}) copy-start(f32[256,128]{1,0:T(8,128)} %get-tuple-element.11) | copy-start | bytes 393220

commit v3 on v2

--- a/solution.py
+++ b/solution.py
@@ -8,6 +8,7 @@
 HD = 128
 TILE = 128
 BLOCK = 2 * TILE
+ONES = 16
 LOG2E = 1.4426950408889634
 FAR_BELOW = -1e30
 MESH = pl.DeviceIdType.MESH
@@ -21,7 +22,7 @@
 
 
 def kernel(heads, ids, mask, q_ref, g_ref, k_ref, v_ref, att_ref, dq_ref, dk_ref, dv_ref,
-           kv, q_rows, g_rows, q_turned, g_turned, bias, terms, maxima, total, top_ref, share_ref, delta_ref,
+           kv, q_rows, g_rows, q_turned, g_turned, terms, maxima, total, top_ref,
            own_part, pair_out, pair_in, outgoing, landed,
            gather_send, gather_recv, share_send, share_recv, pair_send, pair_recv, ring_send, ring_recv):
     factor = HD ** -0.5
@@ -84,11 +85,6 @@
 
             share_copy((RING - offset) % RING, chunk, core).start()
 
-    row = lax.broadcasted_iota(jnp.int32, (TILE, TILE), 0)
-    lane = lax.broadcasted_iota(jnp.int32, (TILE, TILE), 1)
-    bias[0] = jnp.zeros((TILE, TILE), jnp.float32)
-    bias[1] = jnp.where(lane >= row, 0.0, FAR_BELOW)
-    bias[2] = jnp.full((TILE, TILE), FAR_BELOW, jnp.float32)
     for a in range(2):
         for h in range(heads):
             block = pl.ds((a * heads + h) * TILE, TILE)
@@ -96,38 +92,52 @@
             g_block = g_ref[pl.ds(a * TILE, TILE), pl.ds(h * HD, HD)]
             q_rows[block, :] = q_block
             g_rows[block, :] = g_block
-            q_turned[:, block] = q_block.T
-            g_turned[:, block] = g_block.T
-    top_ref[...] = jnp.full_like(top_ref, FAR_BELOW)
-    share_ref[...] = jnp.zeros_like(share_ref)
-    total[...] = jnp.zeros_like(total)
-
-    def bias_block(owner, r, a):
-        state = jnp.where(mask[ids[me * 2 + a], ids[owner * 2 + r]] == 1, 0, 2)
-        state = jnp.where(owner * 2 + r == me * 2 + a, 1, state)
-        one = bias[state]
-        return jnp.concatenate([one] * (BLOCK // TILE), axis=1)
-
-    def forward_unit(owner):
+            scaled = q_block.T.astype(jnp.float32) * (factor * LOG2E)
+            coarse = scaled.astype(jnp.bfloat16)
+            q_turned[:HD, block] = coarse
+            q_turned[HD:, block] = (scaled - coarse.astype(jnp.float32)).astype(jnp.bfloat16)
+            g_turned[:HD, block] = g_block.T
+
+    def bias_of(owner, r, a):
+        return jnp.where(mask[ids[me * 2 + a], ids[owner * 2 + r]] == 1, 0.0, FAR_BELOW)
+
+    def forward_unit(owner, first):
         keys = kv[owner, 0:2].reshape(BLOCK, HD)
-        values_turned = kv[owner, 2:4].reshape(BLOCK, HD).T
-        biases = [jnp.concatenate([bias_block(owner, 0, a), bias_block(owner, 1, a)], axis=0) for a in range(2)]
+        keys = jnp.concatenate([keys, keys], axis=1)
+        values_turned = jnp.concatenate(
+            [kv[owner, 2:4].reshape(BLOCK, HD).T, jnp.ones((ONES, BLOCK), jnp.bfloat16)], axis=0)
+        biases = [[bias_of(owner, r, a) for a in range(2)] for r in range(2)]
+
+        def scores_of(column):
+            return dot(keys, q_turned[:, column])
+
+        ahead = scores_of(columns[0])
         for n, column in enumerate(columns):
-            scores = dot(keys, q_turned[:, column]) * (factor * LOG2E) + biases[n // blocks_per_tile]
-            old = top_ref[:, column]
-            top = jnp.maximum(old, jnp.max(scores, axis=0, keepdims=True))
-            shrink = jnp.exp2(old - top)
-            probs = jnp.exp2(scores - top)
+            scores = ahead
+            if n + 1 < len(columns):
+                ahead = scores_of(columns[n + 1])
+            a = n // blocks_per_tile
+            halves = [scores[r * TILE:(r + 1) * TILE] for r in range(2)]
+            if first:
+                row = lax.broadcasted_iota(jnp.int32, (TILE, BLOCK), 0)
+                lane = lax.broadcasted_iota(jnp.int32, (TILE, BLOCK), 1) % TILE
+                halves[a] = jnp.where(lane >= row, halves[a], FAR_BELOW)
+            tops = [jnp.max(halves[r], axis=0, keepdims=True) + biases[r][a] for r in range(2)]
+            top = jnp.maximum(tops[0], tops[1])
+            if not first:
+                old = top_ref[:, column]
+                top = jnp.maximum(old, top)
+            probs = jnp.concatenate([jnp.exp2(halves[r] - (top - biases[r][a])) for r in range(2)], axis=0)
             terms[owner, :, column] = probs
             maxima[owner, :, column] = top
             top_ref[:, column] = top
-            share_ref[:, column] = share_ref[:, column] * shrink + jnp.sum(probs, axis=0, keepdims=True)
-            total[:, column] = total[:, column] * shrink + dot(values_turned, probs.astype(jnp.bfloat16))
+            weighted = dot(values_turned, probs.astype(jnp.bfloat16))
+            total[:, column] = weighted if first else total[:, column] * jnp.exp2(old - top) + weighted
 
     def forward_step(j, carried):
-        unit = jnp.where(j < 2, j, j - 2)
-
-        @pl.when(jnp.logical_or(j < 2, j >= 4))
+        unit = jnp.where(j < 2, 1, j - 2)
+
+        @pl.when(jnp.logical_or(j == 1, j >= 4))
         def _():
             rest = jnp.maximum(unit - 2, 0)
             near = rest // 4
@@ -143,7 +153,7 @@
                 for chunk in range(4):
                     share_copy(back, chunk, 1 - core).wait_recv()
 
-            forward_unit(((z + RING - back) % RING) * 2 + column)
+            forward_unit(((z + RING - back) % RING) * 2 + column, False)
 
         @pl.when(j < 14)
         def _():
@@ -151,16 +161,25 @@
 
         return carried
 
+    forward_unit(me, True)
     lax.fori_loop(0, 18, forward_step, 0)
 
-    attended = (total[...] / share_ref[...]).astype(jnp.bfloat16)
-    delta_ref[...] = jnp.sum(g_turned[...].astype(jnp.float32) * attended.astype(jnp.float32), axis=0, keepdims=True)
-    top_ref[...] = top_ref[...] + jnp.log2(share_ref[...])
+    attended = (total[:HD] / total[HD:HD + 1]).astype(jnp.bfloat16)
+    rest = -jnp.sum(g_turned[:HD].astype(jnp.float32) * attended.astype(jnp.float32), axis=0, keepdims=True)
+    top_ref[...] = top_ref[...] + jnp.log2(total[HD:HD + 1])
+    place = lax.broadcasted_iota(jnp.int32, (ONES, 1), 0)
+    extra = jnp.zeros((ONES, wide), jnp.float32)
+    for n in range(3):
+        term = rest.astype(jnp.bfloat16).astype(jnp.float32)
+        extra = jnp.where(place == n, term, extra)
+        rest = rest - term
+    g_turned[HD:HD + ONES] = extra.astype(jnp.bfloat16)
+    g_turned[HD + ONES:] = jnp.zeros((HD - ONES, wide), jnp.bfloat16)
     for a in range(2):
         for h in range(heads):
             n = a * heads + h
             att_ref[pl.ds(a * TILE, TILE), pl.ds(h * HD, HD)] = attended[:, n * TILE:(n + 1) * TILE].T
-    total[...] = jnp.zeros_like(total)
+    total[:HD] = jnp.zeros((HD, wide), jnp.float32)
 
     def pair_copy(n):
         return pltpu.make_async_remote_copy(
@@ -187,15 +206,24 @@
 
     def backward_unit(owner):
         keys_turned = kv[owner, 0:2].reshape(BLOCK, HD).T
-        values = kv[owner, 2:4].reshape(BLOCK, HD)
+        values = jnp.concatenate(
+            [kv[owner, 2:4].reshape(BLOCK, HD),
+             (lax.broadcasted_iota(jnp.int32, (BLOCK, HD), 1) < 3).astype(jnp.bfloat16)], axis=1)
         probs_all, dscores_all = [], []
+
+        def dprobs_of(column):
+            return dot(values, g_turned[:, column])
+
+        ahead = dprobs_of(columns[0])
         for n, column in enumerate(columns):
+            dprobs = ahead
+            if n + 1 < len(columns):
+                ahead = dprobs_of(columns[n + 1])
             probs = terms[owner, :, column] * jnp.exp2(maxima[owner, :, column] - top_ref[:, column])
-            dprobs = dot(values, g_turned[:, column])
-            dscores = (probs * (dprobs - delta_ref[:, column])).astype(jnp.bfloat16)
+            dscores = (probs * dprobs).astype(jnp.bfloat16)
             probs_all.append(probs.astype(jnp.bfloat16))
             dscores_all.append(dscores)
-            total[:, column] += dot(keys_turned, dscores)
+            total[:HD, column] += dot(keys_turned, dscores)
         dk = dot(jnp.concatenate(dscores_all, axis=1), q_rows[...]) * factor
         dv = dot(jnp.concatenate(probs_all, axis=1), g_rows[...])
         return dk, dv
@@ -246,7 +274,7 @@
     for a in range(2):
         for h in range(heads):
             n = a * heads + h
-            dq_ref[pl.ds(a * TILE, TILE), pl.ds(h * HD, HD)] = (total[:, n * TILE:(n + 1) * TILE] * factor).T
+            dq_ref[pl.ds(a * TILE, TILE), pl.ds(h * HD, HD)] = (total[:HD, n * TILE:(n + 1) * TILE] * factor).T
 
     pair_copy(7).wait_recv()
     for which, out in ((1, dv_ref), (0, dk_ref)):
@@ -292,14 +320,11 @@
             pltpu.VMEM((devices, 4, TILE, HD), bf16),
             pltpu.VMEM((wide, HD), bf16),
             pltpu.VMEM((wide, HD), bf16),
-            pltpu.VMEM((HD, wide), bf16),
-            pltpu.VMEM((HD, wide), bf16),
-            pltpu.VMEM((3, TILE, TILE), f32),
+            pltpu.VMEM((2 * HD, wide), bf16),
+            pltpu.VMEM((2 * HD, wide), bf16),
             pltpu.VMEM((devices, BLOCK, wide), f32),
             pltpu.VMEM((devices, 1, wide), f32),
-            pltpu.VMEM((HD, wide), f32),
-            pltpu.VMEM((1, wide), f32),
-            pltpu.VMEM((1, wide), f32),
+            pltpu.VMEM((HD + ONES, wide), f32),
             pltpu.VMEM((1, wide), f32),
             pltpu.VMEM((RING, 2, BLOCK, HD), f32),
             pltpu.VMEM((RING, 2, BLOCK, HD), bf16),

time: 63.8 us -> 52.1 us (0.82)
  Pallas kernels: 58.6 us -> 46.9 us
    pallas_call x1, Pallas kernels: 58.6 us -> 46.9 us  [fused(): pl.pallas_call(lambda *refs: kernel(heads, *refs), out_shape=(jax.ShapeDt...]
where the time goes in v3:
time: 52.1 us; the launch traced here: 51.9 us
  Pallas kernels  46.9 us (90%)
  local copies, waits for them, and re-layouts  4.36 us (8%)
  between operations  0.65 us (1%)
    pallas_call x1, Pallas kernels, fused(): pl.pallas_call(lambda *refs: kernel(heads, *refs), out_shape=(jax.ShapeDt...  46.9 us
    unnamed x10, local copies, waits for them, and re-layouts  4.36 us

profile of v3, /device:TPU:2, one launch (start us, length us, event | category | flops | bytes accessed | tf_op | source)
XLA Modules:
  0.0 51.9 jit_solution(4349795999233856164)
XLA Ops:
  0.6 46.9 %fused.1 = (bf16[256,512]{1,0:T(8,128)(2,1)}, f32[256,512]{1,0:T(8,128)}, f32[256,128]{1,0:T(8,128)}, f32[256,128]{1,0:T(8,128)}) custom-call(s32[32]{0:T(128)} %refs_0_.1, s32[32,32]{1,0:T(8,128)} %refs_1_.1, bf16[256,512]{1,0:T(8,128)(2,1)} %refs_2_.1, bf16[256,512]{1,0:T(8,128)(2,1)} %refs_3_.1, bf16[256,128]{1,0:T(8,128)(2,1)} %refs_4_.1, ...), custom_call_target="tpu_custom_call" | custom-call | tf_op jit(solution)/shard_map/fused/pallas_call | solution.py:309
  47.5 0.0 copy-start
  47.5 1.7 %copy.14 = bf16[256,512]{1,0:T(8,128)(2,1)} copy(bf16[256,512]{1,0:T(8,128)(2,1)} %get-tuple-element.8) | data formatting | bytes 524288
  49.3 0.0 copy-done
  49.3 0.0 copy-start.2
  49.3 0.8 %copy.15 = f32[256,512]{1,0:T(8,128)} copy(f32[256,512]{1,0:T(8,128)S(1)} %copy-done) | data formatting | bytes 1048576
  50.1 0.2 copy-done.2
  50.3 0.0 copy-start.1
  50.3 0.7 %copy.16 = f32[256,128]{1,0:T(8,128)} copy(f32[256,128]{1,0:T(8,128)S(1)} %copy-done.2) | data formatting | bytes 262144
  51.0 0.3 copy-done.1
  51.2 0.7 %copy.17 = f32[256,128]{1,0:T(8,128)} copy(f32[256,128]{1,0:T(8,128)S(1)} %copy-done.1) | data formatting | bytes 262144
Async XLA Ops:
  47.5 1.7 %copy-start = (f32[256,512]{1,0:T(8,128)S(1)}, f32[256,512]{1,0:T(8,128)}, u32[]{:S(2)}) copy-start(f32[256,512]{1,0:T(8,128)} %get-tuple-element.9) | copy-start | bytes 1572868
  49.3 1.0 %copy-start.2 = (f32[256,128]{1,0:T(8,128)S(1)}, f32[256,128]{1,0:T(8,128)}, u32[]{:S(2)}) copy-start(f32[256,128]{1,0:T(8,128)} %get-tuple-element.10) | copy-start | bytes 393220
  50.3 1.0 %copy-start.1 = (f32[256,128]{1,0:T(8,128)S(1)}, f32[256,128]{1,0:T(8,128)}, u32[]{:S(2)}) copy-start(f32[256,128]{1,0:T(8,128)} %get-tuple-element.11) | copy-start | bytes 393220
